TPU v7x, 32 devices: a whole 2x2x4 slice. The times are simulated.
32 devices in a mesh: parts: 2 (over y), blk: 16 (over z, x, core).
Axes of the slice: x: 2, y: 2, z: 4, core: 2. Of those that a mesh axis runs over, the one named last changes fastest.
Arguments:
- features: bfloat16 [8192, 128], P(('parts', 'blk')), parts along dimension 0, may hold values from -6 to 6
- w_first: bfloat16 [128, 256], replicated, may hold values from -0.5 to 0.5
- w_second: bfloat16 [256, 8192], replicated, may hold values from -0.375 to 0.375
- panel: bfloat16 [64, 64, 256], P(('parts', 'blk')), parts along dimension 0, may hold values from -6 to 6
- energies: float32 [256], replicated, may hold values from -1 to 1
- pair_dest: int32 [8192, 1], P(('parts', 'blk')), parts along dimension 0, may hold values from 0 to 15, as said below
- pair_row: int32 [8192], P(('parts', 'blk')), parts along dimension 0, may hold values from 0 to 1
- pair_col: int32 [8192], P(('parts', 'blk')), parts along dimension 0, may hold values from 0 to 1
Outputs:
- residual: float32 [64, 64, 256], P(('parts', 'blk')), parts along dimension 0
- loss: float32 [2], P('parts'), parts along dimension 0
- grad_first: float32 [256, 256], P('parts'), parts along dimension 0
- grad_second: float32 [512, 8192], P('parts', 'blk'), parts along dimension 0
There are 2 independent parts, one for each index of `parts`. A program takes and returns all parts, laid end to end along the dimension named above; an argument that names none is the same for every part. Nothing has to cross between parts.
Inputs may be any that keep to these rules, and one draw needn't show every extreme that they name: `pair_dest`: among one device's 256 pairs at most 24 have their block row on one device; every device owns the block rows of exactly 24 of its own pairs. Owners lie mostly near the listing device along the axis.
All inputs are finite; a program needn't handle non-finite values.
Results may differ from a plain program's by a relative error of at most 0.004.
Values may be sent and summed in bfloat16 or wider, within the bound.
No kernel may reach another device: no remote copies, remote signals or barrier semaphores. Data moves between devices by JAX's collectives and lax.ppermute only.
A program may use at most 128 MiB of HBM per device.

v0:
```python
import jax
import jax.numpy as jnp
from jax import lax
from jax.sharding import PartitionSpec as P


def predict(feats, w_first, w_second, orbitals):
    pre = jnp.dot(feats, w_first, preferred_element_type=jnp.float32)
    hidden = jax.nn.silu(pre).astype(jnp.bfloat16)
    blocks = (jnp.dot(hidden, w_second, preferred_element_type=jnp.float32) / orbitals).astype(
        jnp.bfloat16
    )
    return (pre, hidden, blocks)


def weight_terms(feats, pre, hidden, d_flat, w_second, orbitals):
    term_second = jnp.dot(hidden.T, d_flat, preferred_element_type=jnp.float32) / orbitals
    d_hidden = (
        lax.dot_general(
            d_flat, w_second, (((1,), (1,)), ((), ())), preferred_element_type=jnp.float32
        )
        / orbitals
    )
    sig = jax.nn.sigmoid(pre)
    d_pre = (d_hidden * sig * (1.0 + pre * (1.0 - sig))).astype(jnp.bfloat16)
    term_first = jnp.dot(feats.T, d_pre, preferred_element_type=jnp.float32)
    return (term_first, term_second)


def slot_work(slot_blocks, slot_panel, slot_rows, energies, blk_dev, total_blocks):
    slots, unused_two, orbitals, unused_o = slot_blocks.shape
    columns = slot_panel.shape[2]
    group = 32
    steps_count = slots // group
    grouped = (
        slot_blocks.reshape(steps_count, group, 2, orbitals, orbitals),
        slot_panel.reshape(steps_count, group, orbitals, columns),
        slot_rows.reshape(steps_count, group),
    )
    row_ids = jnp.arange(blk_dev, dtype=jnp.int32)

    def forward(total, item):
        blocks, coeffs, rows = item
        h_panel = jnp.einsum(
            "sab,sbp->sap", blocks[:, 0], coeffs, preferred_element_type=jnp.float32
        )
        s_panel = jnp.einsum(
            "sab,sbp->sap", blocks[:, 1], coeffs, preferred_element_type=jnp.float32
        )
        contrib = h_panel - s_panel * energies
        selector = (rows[None, :] == row_ids[:, None]).astype(jnp.float32)
        added = jnp.einsum("rs,sap->rap", selector, contrib, precision=lax.Precision.HIGHEST)
        return (total + added, None)

    residual = lax.scan(forward, jnp.zeros((blk_dev, orbitals, columns), jnp.float32), grouped)[0]
    grad_h = (residual / total_blocks).astype(jnp.bfloat16)
    grad_s = (-(residual * energies) / total_blocks).astype(jnp.bfloat16)

    def backward(carry, item):
        blocks, coeffs, rows = item
        valid = (rows >= 0)[:, None, None]
        safe_rows = jnp.maximum(rows, 0)
        gh_rows = jnp.where(valid, grad_h[safe_rows], jnp.zeros((), jnp.bfloat16))
        gs_rows = jnp.where(valid, grad_s[safe_rows], jnp.zeros((), jnp.bfloat16))
        d_h = jnp.einsum(
            "sap,sbp->sab", gh_rows, coeffs, preferred_element_type=jnp.float32
        ).astype(jnp.bfloat16)
        d_s = jnp.einsum(
            "sap,sbp->sab", gs_rows, coeffs, preferred_element_type=jnp.float32
        ).astype(jnp.bfloat16)
        return (carry, jnp.stack([d_h, d_s], axis=1))

    d_blocks = lax.scan(backward, 0, grouped)[1]
    return (residual, d_blocks.reshape(slots, 2, orbitals, orbitals))


def local(features, w_first, w_second, panel, energies, pair_dest, pair_row, pair_col):
    n_dev = lax.axis_size("blk")
    my_index = lax.axis_index("blk")
    pair_count, feat_width = features.shape
    blk_dev, orbitals, columns = panel.shape
    capacity = 3 * pair_count // (2 * n_dev)
    slots = n_dev * capacity
    total_blocks = blk_dev * n_dev
    dest = pair_dest[:, 0]
    dest_table = (dest[:, None] == jnp.arange(n_dev, dtype=jnp.int32)[None, :]).astype(jnp.int32)
    rank_in = jnp.sum(jnp.cumsum(dest_table, axis=0) * dest_table, axis=1) - 1
    slot_of = dest * capacity + rank_in
    source = (
        jnp.full((slots,), pair_count, jnp.int32)
        .at[slot_of]
        .set(jnp.arange(pair_count, dtype=jnp.int32))
    )
    empty_label = jnp.full((1,), -1, jnp.int32)
    rows_sent = jnp.concatenate([pair_row, empty_label])[source]
    cols_sent = jnp.concatenate([my_index * blk_dev + pair_col, jnp.zeros((1,), jnp.int32)])[source]
    labels = jnp.stack([rows_sent, cols_sent], axis=-1).reshape(n_dev, capacity, 2)
    whole_panel = lax.all_gather(panel, "blk", axis=0, tiled=True)
    pre, hidden, blocks = predict(features, w_first, w_second, orbitals)
    padded = jnp.concatenate([blocks, jnp.zeros((1, blocks.shape[1]), jnp.bfloat16)], axis=0)
    send_blocks = padded[source].reshape(n_dev, capacity, 2, orbitals, orbitals)
    got_blocks, got_labels = (
        lax.all_to_all(send_blocks, "blk", split_axis=0, concat_axis=0, tiled=True),
        lax.all_to_all(labels, "blk", split_axis=0, concat_axis=0, tiled=True),
    )
    got_labels = got_labels.reshape(slots, 2)
    slot_panel = whole_panel[got_labels[:, 1]]
    residual, d_blocks = slot_work(
        got_blocks.reshape(slots, 2, orbitals, orbitals),
        slot_panel,
        got_labels[:, 0],
        energies,
        blk_dev,
        total_blocks,
    )
    back = lax.all_to_all(
        d_blocks.reshape(n_dev, capacity, 2, orbitals, orbitals),
        "blk",
        split_axis=0,
        concat_axis=0,
        tiled=True,
    )
    d_flat = back.reshape(slots, 2 * orbitals * orbitals)[slot_of]
    term_first, term_second = weight_terms(features, pre, hidden, d_flat, w_second, orbitals)
    grad_second = lax.psum_scatter(term_second, "blk", scatter_dimension=1, tiled=True)
    grad_first, square_sum = lax.psum((term_first, jnp.sum(residual * residual)), "blk")
    loss = (square_sum / (total_blocks * orbitals * columns)).reshape(1)
    return (residual, loss, grad_first, grad_second)


def solution(mesh):
    in_specs = (
        P(("parts", "blk"), None),
        P(),
        P(),
        P(("parts", "blk"), None, None),
        P(),
        P(("parts", "blk"), None),
        P(("parts", "blk")),
        P(("parts", "blk")),
    )
    out_specs = (P(("parts", "blk"), None, None), P("parts"), P("parts", None), P("parts", "blk"))
    return jax.shard_map(local, mesh=mesh, in_specs=in_specs, out_specs=out_specs, check_vma=False)
```

profile of v0, /device:TPU:0, one launch (start us, length us, event | category | flops | bytes accessed | tf_op | source)
XLA Modules:
  0.0 824.7 jit_solution(7765582669645620948)
XLA Ops:
  12.3 2.8 gather_fusion.3
  15.9 2.8 gather_fusion.2
  19.4 7.4 all-to-all-start
  27.8 3.5 fusion.35
  31.3 2.5 concatenate.12
  33.7 17.6 %gather_fusion.4 = bf16[384,8192]{1,0:T(8,128)(2,1)} fusion(bf16[257,8192]{1,0:T(8,128)(2,1)} %concatenate.12, s32[1024]{0:T(1024)S(1)} %pad_clamp_fusion.3), kind=kCustom, calls=%fused_computation.4 | custom fusion | bytes 12584448 | tf_op jit(solution)/shard_map/gather | solution.py:101
  51.4 17.9 %reshape.77 = bf16[16,24,2,64,64]{4,3,2,1,0:T(8,128)(2,1)} reshape(bf16[384,8192]{1,0:T(8,128)(2,1)} %gather_fusion.4) | data formatting | bytes 12582912 | tf_op jit(solution)/shard_map/reshape | solution.py:101
  69.2 16.7 %reshape.156 = bf16[16,2,98304]{2,1,0:T(2,128)(2,1)} reshape(bf16[16,24,2,64,64]{4,3,2,1,0:T(8,128)(2,1)} %reshape.77) | data formatting | bytes 12582912
  85.9 6.0 all-to-all-start.1
  92.9 98.0 %all-gather.2.cloned.1.call-done = bf16[32,64,256]{2,1,0:T(8,128)(2,1)} async-done(((bf16[2,64,256]{2,1,0:T(8,128)(2,1)}), bf16[32,64,256]{2,1,0:T(8,128)(2,1)}) %all-gather.2.cloned.1.call-update) | async-done | bytes 1048592 | tf_op jit(solution)/shard_map/all_gather | solution.py:98
  191.0 12.4 %gather_fusion.5 = bf16[384,64,256]{2,1,0:T(8,128)(2,1)} fusion(bf16[32,64,256]{2,1,0:T(8,128)(2,1)} %all-gather.2.cloned.1.call-done, s32[1024]{0:T(1024)S(1)} %pad_clamp_fusion.2), kind=kCustom, calls=%fused_computation.5 | custom fusion | bytes 25167360 | tf_op jit(solution)/shard_map/gather | solution.py:107
  203.4 9.2 %all-to-all-done.1 = bf16[16,2,98304]{2,1,0:T(2,128)(2,1)} async-done(((bf16[16,2,98304]{2,1,0:T(2,128)(2,1)}), bf16[16,2,98304]{2,1,0:T(2,128)(2,1)}, u32[]{:S(2)}, u32[]{:S(2)}) %all-to-all-start.1) | async-done | bytes 6291488 | tf_op jit(solution)/shard_map/all_to_all | solution.py:103
  212.5 16.4 %reshape.157 = bf16[16,24,2,64,64]{4,3,2,1,0:T(8,128)(2,1)} reshape(bf16[16,2,98304]{2,1,0:T(2,128)(2,1)} %all-to-all-done.1) | data formatting | bytes 12582912
  229.0 82.3 %while.22 = (s32[]{:T(128)}, f32[2,64,256]{2,0,1:T(2,128)S(1)}, s32[12,32]{1,0:T(8,128)S(1)}, bf16[12,32,2,64,64]{4,3,2,1,0:T(8,128)(2,1)}, bf16[12,32,64,256]{3...) while((s32[]{:T(128)}, f32[2,64,256]{2,0,1:T(2,128)S(1)}, ...), condition=%wide.region_5.6_spmd.clone, body=%wide.region_4.5_spmd.clone.sunk | while | flops 147914816 | bytes 13372387 | solution.py:55
  231.9 1.7 multiply_subtract_fusion.2
  233.6 2.2 fusion.85
  240.5 2.2 fusion.85
  245.6 1.7 multiply_subtract_fusion.2
  247.3 2.2 fusion.85
  254.2 2.2 fusion.85
  261.1 2.2 fusion.85
  267.9 2.2 fusion.85
  274.8 2.2 fusion.85
  281.7 2.2 fusion.85
  288.5 2.2 fusion.85
  295.4 2.2 fusion.85
  302.3 2.2 fusion.85
  309.1 2.2 fusion.85
  312.1 72.8 %while.21 = (s32[]{:T(128)}, bf16[12,32,2,64,64]{4,3,2,1,0:T(8,128)(2,1)}, s32[12,32]{1,0:T(8,128)S(1)}, bf16[2,64,256]{2,1,0:T(8,128)(2,1)S(1)}, bf16[12,32,64,...) while((s32[]{:T(128)}, bf16[12,32,2,64,64]{4,3,2,1,0:T(8,128)(2,1)}, ...), condition=%wide.region_9.10_spmd, body=%wide.region_8.9_spmd.sunk | while | flops 135791680 | bytes 10492341 | solution.py:73
  312.8 1.7 fusion.77
  315.1 1.7 fusion.78
  318.9 1.7 fusion.77
  321.2 1.7 fusion.78
  324.9 1.7 fusion.77
  327.3 1.7 fusion.78
  331.0 1.7 fusion.77
  333.3 1.7 fusion.78
  337.0 1.7 fusion.77
  339.4 1.7 fusion.78
  343.1 1.7 fusion.77
  345.4 1.7 fusion.78
  349.2 1.7 fusion.77
  351.5 1.7 fusion.78
  355.2 1.7 fusion.77
  357.6 1.7 fusion.78
  361.2 1.7 fusion.77
  363.6 1.7 fusion.78
  367.3 1.7 fusion.77
  369.6 1.7 fusion.78
  373.4 1.7 fusion.77
  375.7 1.7 fusion.78
  379.4 1.7 fusion.77
  381.8 1.7 fusion.78
  384.8 16.6 %reshape.158 = bf16[16,2,98304]{2,1,0:T(2,128)(2,1)} reshape(bf16[16,24,2,64,64]{4,3,2,1,0:T(8,128)(2,1)} %bitcast.100) | data formatting | bytes 12582912
  401.5 28.0 %all-to-all-start.2 = ((bf16[16,2,98304]{2,1,0:T(2,128)(2,1)}), bf16[16,2,98304]{2,1,0:T(2,128)(2,1)}, u32[]{:S(2)}, u32[]{:S(2)}) async-start(bf16[16,2,98304]{2,1,0:T(2,128)(2,1)} %reshape.158), calls=%async_computation.2 | async-start | bytes 12582912 | tf_op jit(solution)/shard_map/all_to_all | solution.py:116
  429.9 113.9 %all-to-all-done.2 = bf16[16,2,98304]{2,1,0:T(2,128)(2,1)} async-done(((bf16[16,2,98304]{2,1,0:T(2,128)(2,1)}), bf16[16,2,98304]{2,1,0:T(2,128)(2,1)}, u32[]{:S(2)}, u32[]{:S(2)}) %all-to-all-start.2) | async-done | bytes 6291488 | tf_op jit(solution)/shard_map/all_to_all | solution.py:116
  543.7 16.3 %reshape.159 = bf16[16,24,2,64,64]{4,3,2,1,0:T(8,128)(2,1)} reshape(bf16[16,2,98304]{2,1,0:T(2,128)(2,1)} %all-to-all-done.2) | data formatting | bytes 12582912
  560.0 17.0 %reshape.80 = bf16[384,8192]{1,0:T(8,128)(2,1)} reshape(bf16[16,24,2,64,64]{4,3,2,1,0:T(8,128)(2,1)} %reshape.159) | data formatting | bytes 12582912 | tf_op jit(solution)/shard_map/reshape | solution.py:123
  577.0 12.6 %gather_fusion.6 = bf16[256,8192]{1,0:T(8,128)(2,1)} fusion(bf16[384,8192]{1,0:T(8,128)(2,1)} %reshape.80, s32[1024]{0:T(1024)S(1)} %pad_clamp_fusion.1), kind=kCustom, calls=%fused_computation.6 | custom fusion | bytes 8389632 | tf_op jit(solution)/shard_map/gather | solution.py:123
  589.6 5.7 convolution_bitcast_fusion
  595.3 6.7 convolution_multiply_fusion
  602.1 56.7 %psum.14 = f32[]{:T(128)} all-reduce(f32[]{:T(128)} %get-tuple-element.172), channel_id=1, replica_groups=mesh['parts'=2,'blk'=16] {'blk'}, use_global_device_ids=true, to_apply=%region_7.8 | all-reduce | flops 1 | bytes 8 | tf_op jit(solution)/shard_map/psum | solution.py:126
  660.1 45.8 %all-reduce.3.cloned.1.call-done = f32[128,256]{0,1:T(8,128)} async-done(((f32[128,256]{0,1:T(8,128)}), f32[128,256]{0,1:T(8,128)}) %all-reduce.3.cloned.1.call-update) | async-done | bytes 131088 | tf_op jit(solution)/shard_map/psum | solution.py:126
  707.6 109.5 %reduce-scatter.2.cloned.1.call-done = f32[256,512]{1,0:T(8,128)} async-done(((f32[256,8192]{1,0:T(8,128)}), f32[256,512]{1,0:T(8,128)}) %reduce-scatter.2.cloned.1.call-update) | async-done | bytes 524304 | tf_op jit(solution)/shard_map/reduce_scatter | solution.py:125
  (161 shorter events, 95.3 us)
Async XLA Ops:
  7.2 19.6 %copy-start = (bf16[256,128]{1,0:T(8,128)(2,1)S(1)}, bf16[256,128]{1,0:T(8,128)(2,1)}, u32[]{:S(2)}) copy-start(bf16[256,128]{1,0:T(8,128)(2,1)} %param.12) | copy-start | bytes 196612
  19.4 66.5 %all-to-all-start = ((s32[16,24,2]{1,2,0:T(2,128)}), s32[16,24,2]{1,2,0:T(2,128)S(1)}, u32[]{:S(2)}, u32[]{:S(2)}) async-start(s32[16,24,2]{1,2,0:T(2,128)} %pad_add_fusion), calls=%async_computation | async-start | bytes 32768 | tf_op jit(solution)/shard_map/all_to_all | solution.py:104
  85.9 126.6 %all-to-all-start.1 = ((bf16[16,2,98304]{2,1,0:T(2,128)(2,1)}), bf16[16,2,98304]{2,1,0:T(2,128)(2,1)}, u32[]{:S(2)}, u32[]{:S(2)}) async-start(bf16[16,2,98304]{2,1,0:T(2,128)(2,1)} %reshape.156), calls=%async_computation.1 | async-start | bytes 12582912 | tf_op jit(solution)/shard_map/all_to_all | solution.py:103
  92.0 99.0 %all-gather.2.cloned.1.call-start = ((), (), s32[]{:S(2)}) async-start(), calls=%async_computation.4 | async-start | bytes 1114112 | tf_op jit(solution)/shard_map/all_gather | solution.py:98
  203.4 25.6 %copy-start.1 = (f32[256]{0:T(256)S(1)}, f32[256]{0:T(256)}, u32[]{:S(2)}) copy-start(f32[256]{0:T(256)} %param.16) | copy-start | bytes 3076
  401.5 142.2 %all-to-all-start.2 = ((bf16[16,2,98304]{2,1,0:T(2,128)(2,1)}), bf16[16,2,98304]{2,1,0:T(2,128)(2,1)}, u32[]{:S(2)}, u32[]{:S(2)}) async-start(bf16[16,2,98304]{2,1,0:T(2,128)(2,1)} %reshape.158), calls=%async_computation.2 | async-start | bytes 12582912 | tf_op jit(solution)/shard_map/all_to_all | solution.py:116
  429.5 276.4 %all-reduce.3.cloned.1.call-start = ((), (), s32[]{:S(2)}) async-start(), calls=%async_computation.5 | async-start | bytes 262144 | tf_op jit(solution)/shard_map/psum | solution.py:126
  595.3 221.8 %reduce-scatter.2.cloned.1.call-start = ((), (), s32[]{:S(2)}) async-start(), calls=%async_computation.6 | async-start | bytes 8912896 | tf_op jit(solution)/shard_map/reduce_scatter | solution.py:125
Sparse Core Ops, SparseCore 0:
  95.0 95.9 all-gather.1
  595.4 110.4 all-reduce.2
  710.5 106.4 reduce-scatter.1
where the time goes:
time: 830 us; the launch traced here: 825 us
  waiting for transfers between devices  377 us (45%)
  local copies, waits for them, and re-layouts  186 us (22%)
  matrix products  124 us (15%)
  blocking collectives  56.7 us (7%)
  starting transfers between devices  42.1 us (5%)
  other arithmetic  21.9 us (3%)
  between operations  15.7 us (2%)
    all_to_all x1, waiting for transfers between devices, local(): lax.all_to_all(d_blocks.reshape(n_dev, capacity, 2, orbitals, orbitals),...  114 us
    reduce_scatter x1, waiting for transfers between devices, local(): lax.psum_scatter(term_second, 'blk', scatter_dimension=1, tiled=True)  109 us
    all_gather x1, waiting for transfers between devices, local(): whole_panel = lax.all_gather(panel, 'blk', axis=0, tiled=True)  98 us
    unnamed x10, local copies, waits for them, and re-layouts  68.4 us
    psum x1, blocking collectives, local(): lax.psum((term_first, jnp.sum(residual * residual)), 'blk')  56.7 us
    psum x1, waiting for transfers between devices, local(): lax.psum((term_first, jnp.sum(residual * residual)), 'blk')  45.8 us
    all_to_all x1, starting transfers between devices, local(): lax.all_to_all(d_blocks.reshape(n_dev, capacity, 2, orbitals, orbitals),...  28 us
    dot_general x12, matrix products, forward(): jnp.einsum('rs,sap->rap', selector, contrib, precision=lax.Precision.HIGH...  26.3 us
  transfers between devices with their start and end apart: 6, of which 5 were waited for; matrix products, arithmetic and copies ran while one was open for 10% of the time, Pallas kernels for 0%

commit v1 on v0

--- a/solution.py
+++ b/solution.py
@@ -2,6 +2,27 @@
 import jax.numpy as jnp
 from jax import lax
 from jax.sharding import PartitionSpec as P
+
+
+def gather_around(array, axis, dim):
+    count, index, rows = (lax.axis_size(axis), lax.axis_index(axis), array.shape[dim])
+    upward = [(i, (i + 1) % count) for i in range(count)]
+    left = [(i, (i - 1) % count) for i in range(count)]
+    out = jnp.zeros((*array.shape[:dim], count * rows, *array.shape[dim + 1 :]), array.dtype)
+    out = lax.dynamic_update_slice_in_dim(out, array, index * rows, axis=dim)
+    from_left = from_right = array
+    halfway = count // 2
+    for lap in range(1, halfway + 1):
+        from_left = lax.ppermute(from_left, axis, upward)
+        out = lax.dynamic_update_slice_in_dim(
+            out, from_left, (index - lap) % count * rows, axis=dim
+        )
+        if lap < count - halfway:
+            from_right = lax.ppermute(from_right, axis, left)
+            out = lax.dynamic_update_slice_in_dim(
+                out, from_right, (index + lap) % count * rows, axis=dim
+            )
+    return out
 
 
 def predict(feats, w_first, w_second, orbitals):
@@ -95,7 +116,7 @@
     rows_sent = jnp.concatenate([pair_row, empty_label])[source]
     cols_sent = jnp.concatenate([my_index * blk_dev + pair_col, jnp.zeros((1,), jnp.int32)])[source]
     labels = jnp.stack([rows_sent, cols_sent], axis=-1).reshape(n_dev, capacity, 2)
-    whole_panel = lax.all_gather(panel, "blk", axis=0, tiled=True)
+    whole_panel = gather_around(panel, "blk", 0)
     pre, hidden, blocks = predict(features, w_first, w_second, orbitals)
     padded = jnp.concatenate([blocks, jnp.zeros((1, blocks.shape[1]), jnp.bfloat16)], axis=0)
     send_blocks = padded[source].reshape(n_dev, capacity, 2, orbitals, orbitals)

time: 830 us -> 868 us (1.046)
  starting transfers between devices: 42.1 us -> 68.8 us
  waiting for transfers between devices: 377 us -> 388 us
    ppermute x0 -> x15, waiting for transfers between devices: none -> 119 us  [the longest x8 119 us: gather_around(): from_left = lax.ppermute(from_left, axis, upward)]
    all_gather x1 -> x0, waiting for transfers between devices: 98 us -> none  [local(): whole_panel = lax.all_gather(panel, 'blk', axis=0, tiled=True)]
    ppermute x0 -> x15, starting transfers between devices: none -> 33.6 us  [the longest x7 31 us: gather_around(): from_right = lax.ppermute(from_right, axis, left)]
    all_to_all x1, waiting for transfers between devices: 9.16 us -> 0.01 us  [local(): lax.all_to_all(send_blocks, 'blk', split_axis=0, concat_axis=0, tiled=True)]
    unnamed x10 -> x12, local copies, waits for them, and re-layouts: 68.4 us -> 68.4 us
  transfers between devices with their start and end apart: 6 -> 20, of which waited for: 5 -> 12; matrix products, arithmetic and copies ran while one was open for 10% -> 9% of each run, Pallas kernels for 0% -> 0%
where the time goes in v1:
time: 868 us; the launch traced here: 862 us
  waiting for transfers between devices  388 us (45%)
  local copies, waits for them, and re-layouts  185 us (21%)
  matrix products  124 us (14%)
  starting transfers between devices  68.8 us (8%)
  blocking collectives  56.7 us (7%)
  other arithmetic  21.8 us (3%)
  between operations  16.1 us (2%)
    ppermute x8, waiting for transfers between devices, gather_around(): from_left = lax.ppermute(from_left, axis, upward)  119 us
    all_to_all x1, waiting for transfers between devices, local(): lax.all_to_all(d_blocks.reshape(n_dev, capacity, 2, orbitals, orbitals),...  114 us
    reduce_scatter x1, waiting for transfers between devices, local(): lax.psum_scatter(term_second, 'blk', scatter_dimension=1, tiled=True)  110 us
    unnamed x12, local copies, waits for them, and re-layouts  68.4 us
    psum x1, blocking collectives, local(): lax.psum((term_first, jnp.sum(residual * residual)), 'blk')  56.7 us
    psum x1, waiting for transfers between devices, local(): lax.psum((term_first, jnp.sum(residual * residual)), 'blk')  45.7 us
    ppermute x7, starting transfers between devices, gather_around(): from_right = lax.ppermute(from_right, axis, left)  31 us
    dot_general x12, matrix products, forward(): jnp.einsum('rs,sap->rap', selector, contrib, precision=lax.Precision.HIGH...  26.3 us
  transfers between devices with their start and end apart: 20, of which 12 were waited for; matrix products, arithmetic and copies ran while one was open for 9% of the time, Pallas kernels for 0%

profile of v1, /device:TPU:0, one launch (start us, length us, event | category | flops | bytes accessed | tf_op | source)
XLA Modules:
  0.0 862.4 jit_solution(5082843586348704089)
XLA Ops:
  13.0 2.8 gather_fusion.2
  15.9 2.8 gather_fusion.3
  19.4 7.4 all-to-all-start
  27.8 3.5 fusion.35
  31.2 2.5 concatenate.12
  33.7 17.6 %gather_fusion.4 = bf16[384,8192]{1,0:T(8,128)(2,1)} fusion(bf16[257,8192]{1,0:T(8,128)(2,1)} %concatenate.12, s32[1024]{0:T(1024)S(1)} %pad_clamp_fusion.3), kind=kCustom, calls=%fused_computation.4 | custom fusion | bytes 12584448 | tf_op jit(solution)/shard_map/gather | solution.py:122
  51.3 17.9 %reshape.77 = bf16[16,24,2,64,64]{4,3,2,1,0:T(8,128)(2,1)} reshape(bf16[384,8192]{1,0:T(8,128)(2,1)} %gather_fusion.4) | data formatting | bytes 12582912 | tf_op jit(solution)/shard_map/reshape | solution.py:122
  69.2 16.7 %reshape.156 = bf16[16,2,98304]{2,1,0:T(2,128)(2,1)} reshape(bf16[16,24,2,64,64]{4,3,2,1,0:T(8,128)(2,1)} %reshape.77) | data formatting | bytes 12582912
  85.9 6.2 all-to-all-start.1
  92.5 4.1 collective-permute-start.1
  96.9 103.2 %collective-permute-done = bf16[2,64,256]{2,1,0:T(8,128)(2,1)S(1)} collective-permute-done((bf16[2,64,256]{2,1,0:T(8,128)(2,1)S(1)}, bf16[2,64,256]{2,1,0:T(8,128)(2,1)S(1)}, u32[]{:S(2)}, u32[]{:S(2)}) %collective-permute-start) | collective-permute-done | bytes 65568 | tf_op jit(solution)/shard_map/ppermute | solution.py:16
  200.1 4.4 collective-permute-start.3
  204.6 2.1 collective-permute-done.2
  206.7 4.4 collective-permute-start.5
  211.2 2.1 collective-permute-done.4
  213.2 4.4 collective-permute-start.7
  217.7 2.1 collective-permute-done.6
  219.8 4.4 collective-permute-start.9
  224.3 2.0 collective-permute-done.8
  226.3 4.5 collective-permute-start.11
  230.8 1.9 collective-permute-done.10
  232.8 4.6 collective-permute-start.13
  239.1 2.2 collective-permute-start.14
  241.9 3.7 collective-permute-done.14
  245.6 11.2 %gather_fusion.5 = bf16[384,64,256]{2,1,0:T(8,128)(2,1)} fusion(bf16[32,64,256]{2,1,0:T(8,128)(2,1)S(1)} %constant_dynamic-update-slice_fusion, s32[1024]{0:T(1024)S(1)} %pad_clamp_fusion.2), kind=kCustom, calls=%fused_computation.5 | custom fusion | bytes 25167360 | tf_op jit(solution)/shard_map/gather | solution.py:128
  256.8 16.4 %reshape.157 = bf16[16,24,2,64,64]{4,3,2,1,0:T(8,128)(2,1)} reshape(bf16[16,2,98304]{2,1,0:T(2,128)(2,1)} %all-to-all-done.1) | data formatting | bytes 12582912
  273.2 82.3 %while.22 = (s32[]{:T(128)}, f32[2,64,256]{2,0,1:T(2,128)S(1)}, s32[12,32]{1,0:T(8,128)S(1)}, bf16[12,32,2,64,64]{4,3,2,1,0:T(8,128)(2,1)}, bf16[12,32,64,256]{3...) while((s32[]{:T(128)}, f32[2,64,256]{2,0,1:T(2,128)S(1)}, ...), condition=%wide.region_5.6_spmd.clone, body=%wide.region_4.5_spmd.clone.sunk | while | flops 147914816 | bytes 13372387 | solution.py:76
  277.8 2.2 fusion.85
  284.7 2.2 fusion.85
  291.5 2.2 fusion.85
  298.4 2.2 fusion.85
  305.2 2.2 fusion.85
  312.1 2.2 fusion.85
  319.0 2.2 fusion.85
  325.8 2.2 fusion.85
  332.7 2.2 fusion.85
  339.6 2.2 fusion.85
  346.4 2.2 fusion.85
  353.3 2.2 fusion.85
  356.2 72.8 %while.21 = (s32[]{:T(128)}, bf16[12,32,2,64,64]{4,3,2,1,0:T(8,128)(2,1)}, s32[12,32]{1,0:T(8,128)S(1)}, bf16[2,64,256]{2,1,0:T(8,128)(2,1)S(1)}, bf16[12,32,64,...) while((s32[]{:T(128)}, bf16[12,32,2,64,64]{4,3,2,1,0:T(8,128)(2,1)}, ...), condition=%wide.region_9.10_spmd, body=%wide.region_8.9_spmd.sunk | while | flops 135791680 | bytes 10492341 | solution.py:94
  356.9 1.7 fusion.77
  359.3 1.7 fusion.78
  371.4 1.7 fusion.78
  377.5 1.7 fusion.78
  383.5 1.7 fusion.78
  389.6 1.7 fusion.78
  399.4 1.7 fusion.77
  401.7 1.7 fusion.78
  413.8 1.7 fusion.78
  417.5 1.7 fusion.77
  419.9 1.7 fusion.78
  423.6 1.7 fusion.77
  425.9 1.7 fusion.78
  429.0 16.6 %reshape.158 = bf16[16,2,98304]{2,1,0:T(2,128)(2,1)} reshape(bf16[16,24,2,64,64]{4,3,2,1,0:T(8,128)(2,1)} %bitcast.100) | data formatting | bytes 12582912
  445.6 21.3 %all-to-all-start.2 = ((bf16[16,2,98304]{2,1,0:T(2,128)(2,1)}), bf16[16,2,98304]{2,1,0:T(2,128)(2,1)}, u32[]{:S(2)}, u32[]{:S(2)}) async-start(bf16[16,2,98304]{2,1,0:T(2,128)(2,1)} %reshape.158), calls=%async_computation.2 | async-start | bytes 12582912 | tf_op jit(solution)/shard_map/all_to_all | solution.py:137
  467.3 113.9 %all-to-all-done.2 = bf16[16,2,98304]{2,1,0:T(2,128)(2,1)} async-done(((bf16[16,2,98304]{2,1,0:T(2,128)(2,1)}), bf16[16,2,98304]{2,1,0:T(2,128)(2,1)}, u32[]{:S(2)}, u32[]{:S(2)}) %all-to-all-start.2) | async-done | bytes 6291488 | tf_op jit(solution)/shard_map/all_to_all | solution.py:137
  581.2 16.3 %reshape.159 = bf16[16,24,2,64,64]{4,3,2,1,0:T(8,128)(2,1)} reshape(bf16[16,2,98304]{2,1,0:T(2,128)(2,1)} %all-to-all-done.2) | data formatting | bytes 12582912
  597.5 17.0 %reshape.80 = bf16[384,8192]{1,0:T(8,128)(2,1)} reshape(bf16[16,24,2,64,64]{4,3,2,1,0:T(8,128)(2,1)} %reshape.159) | data formatting | bytes 12582912 | tf_op jit(solution)/shard_map/reshape | solution.py:144
  614.5 12.5 %gather_fusion.6 = bf16[256,8192]{1,0:T(8,128)(2,1)} fusion(bf16[384,8192]{1,0:T(8,128)(2,1)} %reshape.80, s32[1024]{0:T(1024)S(1)} %pad_clamp_fusion.1), kind=kCustom, calls=%fused_computation.6 | custom fusion | bytes 8389632 | tf_op jit(solution)/shard_map/gather | solution.py:144
  627.0 5.7 convolution_bitcast_fusion
  632.8 6.7 convolution_multiply_fusion
  639.5 56.7 %psum.14 = f32[]{:T(128)} all-reduce(f32[]{:T(128)} %get-tuple-element.172), channel_id=1, replica_groups=mesh['parts'=2,'blk'=16] {'blk'}, use_global_device_ids=true, to_apply=%region_7.8 | all-reduce | flops 1 | bytes 8 | tf_op jit(solution)/shard_map/psum | solution.py:147
  697.5 45.7 %all-reduce.3.cloned.1.call-done = f32[128,256]{0,1:T(8,128)} async-done(((f32[128,256]{0,1:T(8,128)}), f32[128,256]{0,1:T(8,128)}) %all-reduce.3.cloned.1.call-update) | async-done | bytes 131088 | tf_op jit(solution)/shard_map/psum | solution.py:147
  744.9 109.5 %reduce-scatter.2.cloned.1.call-done = f32[256,512]{1,0:T(8,128)} async-done(((f32[256,8192]{1,0:T(8,128)}), f32[256,512]{1,0:T(8,128)}) %reduce-scatter.2.cloned.1.call-update) | async-done | bytes 524304 | tf_op jit(solution)/shard_map/reduce_scatter | solution.py:146
  (206 shorter events, 119.7 us)
Async XLA Ops:
  7.2 19.6 %copy-start = (bf16[256,128]{1,0:T(8,128)(2,1)S(1)}, bf16[256,128]{1,0:T(8,128)(2,1)}, u32[]{:S(2)}) copy-start(bf16[256,128]{1,0:T(8,128)(2,1)} %param.12) | copy-start | bytes 196612
  19.4 66.5 %all-to-all-start = ((s32[16,24,2]{1,2,0:T(2,128)}), s32[16,24,2]{1,2,0:T(2,128)S(1)}, u32[]{:S(2)}, u32[]{:S(2)}) async-start(s32[16,24,2]{1,2,0:T(2,128)} %pad_add_fusion), calls=%async_computation | async-start | bytes 32768 | tf_op jit(solution)/shard_map/all_to_all | solution.py:125
  85.9 6.2 copy-start.1
  85.9 170.8 %all-to-all-start.1 = ((bf16[16,2,98304]{2,1,0:T(2,128)(2,1)}), bf16[16,2,98304]{2,1,0:T(2,128)(2,1)}, u32[]{:S(2)}, u32[]{:S(2)}) async-start(bf16[16,2,98304]{2,1,0:T(2,128)(2,1)} %reshape.156), calls=%async_computation.1 | async-start | bytes 12582912 | tf_op jit(solution)/shard_map/all_to_all | solution.py:124
  92.1 108.0 %collective-permute-start = (bf16[2,64,256]{2,1,0:T(8,128)(2,1)S(1)}, bf16[2,64,256]{2,1,0:T(8,128)(2,1)S(1)}, u32[]{:S(2)}, u32[]{:S(2)}) collective-permute-start(bf16[2,64,256]{2,1,0:T(8,128)(2,1)S(1)} %copy-done.1), channel_id=1, source_target_pairs={{0,1},{1,2},{2,3},{3,4},{4,5},{5,6},{6,7},{7,8},{8,9},{9,10},{10,1... | collective-permute-start | bytes 196616 | tf_op jit(solution)/shard_map/ppermute | solution.py:16
  92.5 107.6 %collective-permute-start.1 = (bf16[2,64,256]{2,1,0:T(8,128)(2,1)S(1)}, bf16[2,64,256]{2,1,0:T(8,128)(2,1)S(1)}, u32[]{:S(2)}, u32[]{:S(2)}) collective-permute-start(bf16[2,64,256]{2,1,0:T(8,128)(2,1)S(1)} %copy-done.1), channel_id=1, source_target_pairs={{0,15},{1,0},{2,1},{3,2},{4,3},{5,4},{6,5},{7,6},{8,7},{9,8},{10,9... | collective-permute-start | bytes 196616 | tf_op jit(solution)/shard_map/ppermute | solution.py:21
  200.1 6.6 collective-permute-start.2
  200.1 6.6 collective-permute-start.3
  206.7 6.5 collective-permute-start.4
  206.7 6.5 collective-permute-start.5
  213.2 6.5 collective-permute-start.6
  213.2 6.5 collective-permute-start.7
  219.8 6.5 collective-permute-start.8
  219.8 6.5 collective-permute-start.9
  226.3 6.5 collective-permute-start.10
  226.3 6.5 collective-permute-start.11
  232.8 6.4 collective-permute-start.12
  232.8 9.1 %collective-permute-start.13 = (bf16[2,64,256]{2,1,0:T(8,128)(2,1)S(1)}, bf16[2,64,256]{2,1,0:T(8,128)(2,1)S(1)}, u32[]{:S(2)}, u32[]{:S(2)}) collective-permute-start(bf16[2,64,256]{2,1,0:T(8,128)(2,1)S(1)} %collective-permute-done.11), channel_id=1, source_target_pairs={{0,15},{1,0},{2,1},{3,2},{4,3},{5,4},{6,5},{7,6},{8,7},{9,8},{10,9... | collective-permute-start | bytes 196616 | tf_op jit(solution)/shard_map/ppermute | solution.py:21
  239.1 6.4 collective-permute-start.14
  256.7 16.4 %copy-start.2 = (f32[256]{0:T(256)S(1)}, f32[256]{0:T(256)}, u32[]{:S(2)}) copy-start(f32[256]{0:T(256)} %param.16) | copy-start | bytes 3076
  445.6 135.5 %all-to-all-start.2 = ((bf16[16,2,98304]{2,1,0:T(2,128)(2,1)}), bf16[16,2,98304]{2,1,0:T(2,128)(2,1)}, u32[]{:S(2)}, u32[]{:S(2)}) async-start(bf16[16,2,98304]{2,1,0:T(2,128)(2,1)} %reshape.158), calls=%async_computation.2 | async-start | bytes 12582912 | tf_op jit(solution)/shard_map/all_to_all | solution.py:137
  467.0 276.3 %all-reduce.3.cloned.1.call-start = ((), (), s32[]{:S(2)}) async-start(), calls=%async_computation.4 | async-start | bytes 262144 | tf_op jit(solution)/shard_map/psum | solution.py:147
  632.7 221.7 %reduce-scatter.2.cloned.1.call-start = ((), (), s32[]{:S(2)}) async-start(), calls=%async_computation.5 | async-start | bytes 8912896 | tf_op jit(solution)/shard_map/reduce_scatter | solution.py:146
Sparse Core Ops, SparseCore 0:
  632.8 110.3 all-reduce.2
  747.9 106.4 reduce-scatter.1
